TPU v7x, 32 devices: a whole 2x2x4 slice. The times are simulated.
32 devices in a mesh: row: 8 (over z, y), col: 4 (over x, core).
Axes of the slice: x: 2, y: 2, z: 4, core: 2. Of those that a mesh axis runs over, the one named last changes fastest.
Arguments:
- points: float32 [8, 32768], P(None, ('row', 'col')), may hold values from -4 to 4
- lengthscale: float32 [8], replicated, may hold values from 0.7 to 1.4
- noise: float32 [1], replicated, may hold values from 0.1 to 1
- iterate: float32 [16, 32768], P(None, ('row', 'col')), may hold values from -6 to 6
- residual: float32 [16, 32768], P(None, ('row', 'col')), may hold values from -8 to 8
- direction: float32 [16, 32768], P(None, ('row', 'col')), may hold values from -8 to 8
- previous_rz: float32 [16], replicated, may hold values from 32768 to 131072
- members: int32 [32, 2048], replicated, may hold values from 0 to 32768, as said below
- slot_cluster: int32 [32], P('row'), may hold values from 0 to 31, as said below
- factors: bfloat16 [32, 2048, 2048], P('row', None, 'col'), may hold values from -1 to 3, as said below
Outputs:
- new_iterate: float32 [16, 32768], P(None, ('row', 'col'))
- new_residual: float32 [16, 32768], P(None, ('row', 'col'))
- new_direction: float32 [16, 32768], P(None, ('row', 'col'))
- rz_new: float32 [16], replicated
Inputs may be any that keep to these rules, and one draw needn't show every extreme that they name: `members`: the first 1024 entries of row c are the points c * 1024 to c * 1024 + 1023 in increasing order, the points cluster c owns. They are followed by margin points of one other cluster, distinct from each other, and then by padding entries equal to 32768. Some row has no padding. `slot_cluster`: A permutation of the clusters in which some slot s holds cluster s. `factors`: each slot's matrix is lower triangular with a diagonal of 1 or more.
All inputs are finite; a program needn't handle non-finite values.
Results may differ from a plain program's by a relative error of at most 0.0047.
Values may be sent and summed in bfloat16 or wider, within the bound.
A program may use at most 192 MiB of HBM per device.

v0:
```python
import jax
import jax.numpy as jnp
from jax import lax
from jax.sharding import PartitionSpec as P

CORE = 1024


def kernel_block(left_points, right_points):
    cross_terms = lax.dot_general(
        left_points,
        right_points,
        (((0,), (0,)), ((), ())),
        precision=lax.Precision.HIGHEST,
        preferred_element_type=jnp.float32,
    )
    left_norms = jnp.sum(left_points * left_points, axis=0)
    right_norms = jnp.sum(right_points * right_points, axis=0)
    squared = jnp.maximum(left_norms[:, None] + right_norms[None, :] - 2.0 * cross_terms, 0.0)
    radius = jnp.sqrt(5.0 * squared)
    return ((1.0 + radius + radius * radius / 3.0) * jnp.exp(-radius)).astype(jnp.bfloat16)


def apply_tile(left_points, columns, vectors):
    kernel_tile = kernel_block(left_points, columns)
    return lax.dot_general(
        vectors.astype(jnp.bfloat16),
        kernel_tile,
        (((1,), (1,)), ((), ())),
        preferred_element_type=jnp.float32,
    )


def on_device(
    points,
    lengthscale,
    noise,
    iterate,
    residual,
    direction,
    previous_rz,
    members,
    slot_cluster,
    factors,
):
    scaled = points / lengthscale[:, None]
    probes, own_count = direction.shape
    row_points = lax.all_gather(scaled, "col", axis=1, tiled=True)
    column_terms = apply_tile(
        row_points,
        lax.all_gather(scaled, "row", axis=1, tiled=True),
        lax.all_gather(direction, "row", axis=1, tiled=True),
    )
    partial_value = lax.psum_scatter(column_terms, "col", scatter_dimension=1, tiled=True)
    kernel_image = partial_value + noise[0] * direction
    curvature = lax.psum(jnp.sum(direction * kernel_image, axis=1), ("row", "col"))
    step_size = previous_rz / curvature
    new_iterate = iterate + step_size[:, None] * direction
    new_residual = residual - step_size[:, None] * kernel_image
    residual_low = new_residual.astype(jnp.bfloat16)
    gathered = lax.all_gather(residual_low, ("row", "col"), axis=1, tiled=True)
    point_count = gathered.shape[1]
    padded = jnp.concatenate([gathered, jnp.zeros((probes, 1), jnp.bfloat16)], axis=1)
    member_ids = jnp.take(members, slot_cluster, axis=0)
    present = member_ids < point_count
    own_width = factors.shape[2]
    column_offset = lax.axis_index("col") * own_width
    own_ids = lax.dynamic_slice_in_dim(member_ids, column_offset, own_width, 1)
    selected = jnp.take(padded, own_ids, axis=1)
    inner_part = jnp.einsum("sij,psj->spi", factors, selected, preferred_element_type=jnp.float32)
    inner_sum = lax.psum(inner_part, "col")
    inner_low = jnp.where(present[:, None, :], inner_sum, 0.0).astype(jnp.bfloat16)
    outer_values = jnp.einsum(
        "spi,sij->psj", inner_low, factors, preferred_element_type=jnp.float32
    )
    position = column_offset + jnp.arange(own_width, dtype=jnp.int32)
    is_core = position < CORE
    target_ids = jnp.where(is_core[None, :], own_ids, point_count)
    device_count = lax.axis_size(("row", "col"))
    capacity = min(own_width, own_count) * max(1, own_count // CORE)
    flat_ids = target_ids.reshape(-1)
    target_device = flat_ids // own_count
    matches = (target_device[:, None] == jnp.arange(device_count, dtype=jnp.int32)[None, :]).astype(
        jnp.int32
    )
    ranks = jnp.sum((jnp.cumsum(matches, axis=0) - 1) * matches, axis=1)
    dropped = device_count * capacity
    bucket_index = jnp.where(flat_ids < point_count, target_device * capacity + ranks, dropped)
    flat_values = jnp.transpose(outer_values.reshape(probes, -1))
    value_buckets = jnp.zeros((dropped + 1, probes), jnp.float32).at[bucket_index].set(flat_values)
    id_buckets = jnp.full((dropped + 1,), point_count, jnp.int32).at[bucket_index].set(flat_ids)
    send_values = value_buckets[:dropped].reshape(device_count, capacity * probes)
    send_ids = id_buckets[:dropped].reshape(device_count, capacity)
    got_values, got_ids = (
        lax.all_to_all(send_values, ("row", "col"), split_axis=0, concat_axis=0, tiled=True),
        lax.all_to_all(send_ids, ("row", "col"), split_axis=0, concat_axis=0, tiled=True),
    )
    local_ids = got_ids.reshape(-1) - lax.axis_index(("row", "col")) * own_count
    valid = (local_ids >= 0) & (local_ids < own_count)
    local_ids = jnp.where(valid, local_ids, own_count).astype(jnp.int32)
    received = got_values.reshape(device_count * capacity, probes)
    landed = jnp.zeros((own_count + 1, probes), jnp.float32).at[local_ids].add(received)
    precond = jnp.transpose(landed[:own_count])
    rz_new = lax.psum(jnp.sum(residual_low.astype(jnp.float32) * precond, axis=1), ("row", "col"))
    conjugacy = rz_new / previous_rz
    new_direction = precond + conjugacy[:, None] * direction
    return (new_iterate, new_residual, new_direction, rz_new)


def solution(mesh):
    placed = (
        P(None, ("row", "col")),
        P(),
        P(),
        P(None, ("row", "col")),
        P(None, ("row", "col")),
        P(None, ("row", "col")),
        P(),
        P(),
        P("row"),
        P("row", None, "col"),
    )
    return jax.shard_map(
        on_device,
        mesh=mesh,
        in_specs=placed,
        out_specs=(P(None, ("row", "col")), P(None, ("row", "col")), P(None, ("row", "col")), P()),
        check_vma=False,
    )
```

profile of v0, /device:TPU:0, one launch (start us, length us, event | category | flops | bytes accessed | tf_op | source)
XLA Modules:
  0.0 684.7 jit_solution(15322072037831500532)
XLA Ops:
  7.2 0.9 broadcast_divide_fusion
  8.1 6.5 all_gather.12
  14.6 31.6 %all_gather.13 = f32[8,8192]{1,0:T(8,128)S(1)} all-gather(f32[8,1024]{1,0:T(8,128)S(1)} %broadcast_divide_fusion), channel_id=1, replica_groups=mesh['row'=8,'col'=4] {'row'}, dimensions={1}, use_global_device_ids=true | all-gather | bytes 294912 | tf_op jit(solution)/shard_map/all_gather | solution.py:51
  46.3 0.8 convert.2
  47.1 30.7 %all_gather.14 = bf16[16,8192]{1,0:T(8,128)(2,1)S(1)} all-gather(bf16[16,1024]{1,0:T(8,128)(2,1)S(1)} %convert.2), channel_id=1, replica_groups=mesh['row'=8,'col'=4] {'row'}, dimensions={1}, use_global_device_ids=true | all-gather | bytes 294912 | tf_op jit(solution)/shard_map/all_gather | solution.py:52
  77.9 191.2 %multiply_convert_fusion = bf16[4096,8192]{1,0:T(8,128)(2,1)} fusion(f32[8,4096]{1,0:T(8,128)S(1)} %all_gather.12, f32[8,8192]{1,0:T(8,128)S(1)} %all_gather.13, f32[8192]{0:T(1024)S(1)} %multiply_reduce_fusion, f32[4096]{0:T(1024)S(1)} %multiply_reduce_fusion.1), kind=kOutput, calls=%fused_computation.5 | convolution fusion | flops 3623878656 | bytes 67551232 | tf_op jit(solution)/shard_map/dot_general | solution.py:10
  269.1 26.3 %convolution_bitcast_fusion = f32[16,4096]{1,0:T(8,128)} fusion(bf16[4096,8192]{1,0:T(8,128)(2,1)} %multiply_convert_fusion, bf16[16,8192]{1,0:T(8,128)(2,1)S(1)} %all_gather.14), kind=kOutput, calls=%fused_computation.6 | convolution fusion | flops 1073741824 | bytes 67633152 | tf_op jit(solution)/shard_map/dot_general | solution.py:26
  296.9 19.5 %reduce-scatter.2.cloned.1.call-done = f32[16,1024]{1,0:T(8,128)} async-done(((f32[16,4096]{1,0:T(8,128)}), f32[16,1024]{1,0:T(8,128)}) %reduce-scatter.2.cloned.1.call-update) | async-done | bytes 65552 | tf_op jit(solution)/shard_map/reduce_scatter | solution.py:54
  316.4 1.0 multiply_reduce_fusion.2
  317.4 39.3 %psum.21 = f32[16]{0:T(128)S(1)} all-reduce(f32[16]{0:T(128)S(1)} %multiply_reduce_fusion.2), channel_id=1, replica_groups=mesh['row'=8,'col'=4] {'row','col'}, use_global_device_ids=true, to_apply=%region_4.0 | all-reduce | flops 16 | bytes 128 | tf_op jit(solution)/shard_map/psum | solution.py:56
  356.7 1.6 fusion.25
  358.4 9.1 %reduce-window.6 = s32[32,16,128]{2,1,0:T(8,128)S(1)} reduce-window(s32[32,16,128]{2,1,0:T(8,128)S(1)} %fusion.8, s32[]{:T(128)} %constant.43.clone.1), window={size=1x1x128 pad=0_0x0_0x127_0}, to_apply=%region_5.6 | reduce-window | flops 8323072 | bytes 524292 | tf_op jit(solution)/shard_map/reduce-window
  368.4 8.1 %scatter_custom_fusion = s32[16385]{0:T(1024)S(1)} fusion(s32[2048]{0:T(1024)S(1)} %bitcast.73, s32[2048]{0:T(1024)S(1)} %bitcast.71, s32[]{:T(128)} %constant.33.clone.1), kind=kCustom, calls=%fused_computation.39 | custom fusion | bytes 65544 | tf_op jit(solution)/shard_map/scatter | solution.py:91
  377.1 5.3 all-to-all-start
  382.5 7.5 %all-to-all-done = s32[32,1,512]{2,1,0:T(1,128)S(1)} async-done(((s32[32,1,512]{2,1,0:T(1,128)}), s32[32,1,512]{2,1,0:T(1,128)S(1)}, u32[]{:S(2)}, u32[]{:S(2)}) %all-to-all-start) | async-done | bytes 65568 | tf_op jit(solution)/shard_map/all_to_all | solution.py:96
  390.0 22.9 %all-gather.2.cloned.1.call-done = bf16[16,32768]{1,0:T(8,128)(2,1)} async-done(((bf16[16,1024]{1,0:T(8,128)(2,1)}), bf16[16,32768]{1,0:T(8,128)(2,1)}) %all-gather.2.cloned.1.call-update) | async-done | bytes 1048592 | tf_op jit(solution)/shard_map/all_gather | solution.py:61
  412.9 7.2 %copy.31 = bf16[16,32768]{0,1:T(8,128)(2,1)} copy(bf16[16,32768]{1,0:T(8,128)(2,1)} %all-gather.2.cloned.1.call-done) | data formatting | bytes 2097152
  420.1 9.0 %concatenate.3.clone = bf16[16,32769]{0,1:T(8,128)(2,1)} pad(bf16[16,32768]{0,1:T(8,128)(2,1)} %copy.31, bf16[]{:T(256)} %constant.98.clone.1), padding=0_0x0_1 | pad | bytes 2097186 | tf_op jit(solution)/shard_map/concatenate | solution.py:63
  429.1 10.1 %gather_fusion.1 = bf16[2048,16]{1,0:T(8,128)(2,1)S(1)} fusion(bf16[16,32769]{0,1:T(8,128)(2,1)} %concatenate.3.clone, s32[2048]{0:T(1024)S(1)} %broadcast_clamp_fusion), kind=kCustom, calls=%fused_computation.1 | custom fusion | bytes 139264 | tf_op jit(solution)/shard_map/jit(_take)/gather | solution.py:69
  439.4 5.7 fusion.11
  445.1 17.0 %all-reduce.2 = bf16[4,16,2048]{2,1,0:T(8,128)(2,1)S(1)} all-reduce(f32[4,16,2048]{2,1,0:T(8,128)S(1)} %fusion.11), channel_id=1, replica_groups=mesh['row'=8,'col'=4] {'col'}, use_global_device_ids=true, to_apply=%region_9.10 | all-reduce | flops 131072 | bytes 786432 | tf_op jit(solution)/shard_map/psum | solution.py:71
  462.1 4.6 convolution_bitcast_fusion.1
  467.0 9.3 %scatter_custom_fusion.1 = f32[16385,16]{1,0:T(8,128)} fusion(s32[2048]{0:T(1024)S(1)} %bitcast.74, f32[2048,16]{1,0:T(8,128)S(1)} %copy.26, f32[]{:T(128)} %constant.28.clone.1), kind=kCustom, calls=%fused_computation.7 | custom fusion | bytes 1048644 | tf_op jit(solution)/shard_map/scatter | solution.py:90
  476.3 5.7 slice.27
  482.0 6.9 %all_to_all.16 = f32[32,1,8192]{2,1,0:T(1,128)} reshape(f32[16384,16]{1,0:T(8,128)} %slice.27) | data formatting | bytes 2097152 | tf_op jit(solution)/shard_map/all_to_all | solution.py:95
  488.9 3.6 all-to-all-start.1
  492.7 26.1 %all-to-all-done.1 = f32[32,1,8192]{2,1,0:T(1,128)S(1)} async-done(((f32[32,1,8192]{2,1,0:T(1,128)}), f32[32,1,8192]{2,1,0:T(1,128)S(1)}, u32[]{:S(2)}, u32[]{:S(2)}) %all-to-all-start.1) | async-done | bytes 1048608 | tf_op jit(solution)/shard_map/all_to_all | solution.py:95
  518.8 2.6 reduce
  521.4 4.9 reshape.272
  526.2 112.0 %scatter_custom_fusion.2 = f32[1025,16]{1,0:T(8,128)S(1)} fusion(s32[16384]{0:T(1024)S(1)} %bitcast.67, f32[16384,16]{1,0:T(8,128)} %reshape.272, f32[]{:T(128)} %constant.28.clone.1), kind=kCustom, calls=%fused_computation.12 | custom fusion | flops 262144 | bytes 66112 | tf_op jit(solution)/shard_map/scatter-add | solution.py:102
  638.6 38.5 %psum.23 = f32[16]{0:T(128)S(1)} all-reduce(f32[16]{0:T(128)S(1)} %fusion.10), channel_id=1, replica_groups=mesh['row'=8,'col'=4] {'row','col'}, use_global_device_ids=true, to_apply=%region_13.14 | all-reduce | flops 16 | bytes 128 | tf_op jit(solution)/shard_map/psum | solution.py:104
  677.1 0.7 bitcast_add_fusion
  (55 shorter events, 3.5 us)
Async XLA Ops:
  7.2 289.1 %copy-start = (s32[32,2048]{1,0:T(8,128)S(1)}, s32[32,2048]{1,0:T(8,128)}, u32[]{:S(2)}) copy-start(s32[32,2048]{1,0:T(8,128)} %param.17) | copy-start | bytes 786436
  7.2 309.2 %reduce-scatter.2.cloned.1.call-start = ((), (), s32[]{:S(2)}) async-start(), calls=%async_computation.3 | async-start | bytes 327680 | tf_op jit(solution)/shard_map/reduce_scatter | solution.py:54
  269.1 26.4 %copy-start.5 = (s32[4]{0:T(128)S(1)}, s32[4]{0:T(128)}, u32[]{:S(2)}) copy-start(s32[4]{0:T(128)} %param.18) | copy-start | bytes 52
  269.1 47.3 %copy-start.1 = (f32[16,1024]{1,0:T(8,128)S(1)}, f32[16,1024]{1,0:T(8,128)}, u32[]{:S(2)}) copy-start(f32[16,1024]{1,0:T(8,128)} %param.15) | copy-start | bytes 196612
  269.1 87.6 %copy-start.6 = (f32[16]{0:T(128)S(1)}, f32[16]{0:T(128)}, u32[]{:S(2)}) copy-start(f32[16]{0:T(128)} %param.16) | copy-start | bytes 196
  269.1 87.6 %copy-start.3 = (f32[16,1024]{1,0:T(8,128)S(1)}, f32[16,1024]{1,0:T(8,128)}, u32[]{:S(2)}) copy-start(f32[16,1024]{1,0:T(8,128)} %param.14) | copy-start | bytes 196612
  269.1 87.6 %copy-start.4 = (f32[16,1024]{1,0:T(8,128)S(1)}, f32[16,1024]{1,0:T(8,128)}, u32[]{:S(2)}) copy-start(f32[16,1024]{1,0:T(8,128)} %param.13) | copy-start | bytes 196612
  295.4 117.4 %all-gather.2.cloned.1.call-start = ((), (), s32[]{:S(2)}) async-start(), calls=%async_computation.4 | async-start | bytes 1081344 | tf_op jit(solution)/shard_map/all_gather | solution.py:61
  358.3 280.2 %copy-start.2 = (bf16[16,1024]{1,0:T(8,128)(2,1)S(1)}, bf16[16,1024]{1,0:T(8,128)(2,1)}, u32[]{:S(2)}) copy-start(bf16[16,1024]{1,0:T(8,128)(2,1)} %get-tuple-element.6) | copy-start | bytes 98308
  377.1 12.9 %all-to-all-start = ((s32[32,1,512]{2,1,0:T(1,128)}), s32[32,1,512]{2,1,0:T(1,128)S(1)}, u32[]{:S(2)}, u32[]{:S(2)}) async-start(s32[32,1,512]{2,1,0:T(1,128)} %bitcast.7), calls=%async_computation.1 | async-start | bytes 131072 | tf_op jit(solution)/shard_map/all_to_all | solution.py:96
  488.9 29.8 %all-to-all-start.1 = ((f32[32,1,8192]{2,1,0:T(1,128)}), f32[32,1,8192]{2,1,0:T(1,128)S(1)}, u32[]{:S(2)}, u32[]{:S(2)}) async-start(f32[32,1,8192]{2,1,0:T(1,128)} %all_to_all.16), calls=%async_computation.2 | async-start | bytes 2097152 | tf_op jit(solution)/shard_map/all_to_all | solution.py:95
  677.1 0.7 copy-start.7
Sparse Core Ops, SparseCore 0:
  295.6 20.7 reduce-scatter.1
  358.5 54.3 all-gather.1
where the time goes:
time: 686 us; the launch traced here: 685 us
  matrix products  228 us (33%)
  blocking collectives  164 us (24%)
  other arithmetic  130 us (19%)
  waiting for transfers between devices  76 us (11%)
  local copies, waits for them, and re-layouts  63.6 us (9%)
  between operations  15 us (2%)
  starting transfers between devices  9.04 us (1%)
    dot_general x1, matrix products, kernel_block(): lax.dot_general(left_points, right_points, (((0,), (0,)), ((), ())), prec...  191 us
    scatter-add x1, other arithmetic, on_device(): jnp.zeros((own_count + 1, probes), jnp.float32).at[local_ids].add(received)  112 us
    psum x1, blocking collectives, on_device(): lax.psum(jnp.sum(direction * kernel_image, axis=1), ('row', 'col'))  39.3 us
    psum x1, blocking collectives, on_device(): lax.psum(jnp.sum(residual_low.astype(jnp.float32) * precond, axis=1), ('r...  38.5 us
    all_gather x1, blocking collectives, on_device(): lax.all_gather(scaled, 'row', axis=1, tiled=True)  31.6 us
    all_gather x1, blocking collectives, on_device(): lax.all_gather(direction, 'row', axis=1, tiled=True)  30.7 us
    dot_general x1, matrix products, apply_tile(): lax.dot_general(vectors.astype(jnp.bfloat16), kernel_tile, (((1,), (1,)),...  26.3 us
    all_to_all x1, waiting for transfers between devices, on_device(): lax.all_to_all(send_values, ('row', 'col'), split_axis=0, concat_axis=0,...  26.1 us
  transfers between devices with their start and end apart: 4, of which 4 were waited for; matrix products, arithmetic and copies ran while one was open for 3% of the time, Pallas kernels for 0%

commit v1 on v0

v1 whole, which is shorter than its diff:
```python
import math

import jax
import jax.numpy as jnp
from jax import lax
from jax.experimental import pallas as pl
from jax.experimental.pallas import tpu as pltpu
from jax.sharding import PartitionSpec as P

CORE = 1024
MESH = pl.DeviceIdType.MESH
FEATURES = 64
LOG2E = math.log2(math.e)
SPREAD = math.sqrt(5.0) * LOG2E
SHIFT = 1.5 * LOG2E
LIFT = 0.75 * LOG2E * LOG2E
EXPONENT = -math.log2(3.0 * LOG2E * LOG2E)


def exchange(arrays, collective_id):
    sizes = {axis: lax.axis_size(axis) for _, axis, _ in arrays}
    count = len(arrays)
    widest = max(sizes.values())

    def kernel(*refs):
        sources, targets = refs[:count], refs[count : 2 * count]
        send_sem, recv_sem = refs[2 * count :]
        barrier = pltpu.get_barrier_semaphore()
        for axis, size in sizes.items():
            me = lax.axis_index(axis)
            for offset in range(1, size):
                pl.semaphore_signal(
                    barrier,
                    inc=1,
                    device_id={axis: lax.rem(me + offset, size)},
                    device_id_type=MESH,
                )
        pl.semaphore_wait(barrier, sum(size - 1 for size in sizes.values()))
        copies = []
        for offset in range(1, widest):
            for k, (_, axis, mode) in enumerate(arrays):
                size = sizes[axis]
                if offset >= size:
                    continue
                me = lax.axis_index(axis)
                peer = lax.rem(me + offset, size)
                copy = pltpu.make_async_remote_copy(
                    src_ref=sources[k] if mode == "gather" else sources[k].at[peer],
                    dst_ref=targets[k].at[me],
                    send_sem=send_sem.at[k, offset],
                    recv_sem=recv_sem.at[k, offset],
                    device_id={axis: peer},
                    device_id_type=MESH,
                )
                copy.start()
                copies.append(copy)
        for k, (_, axis, mode) in enumerate(arrays):
            me = lax.axis_index(axis)
            targets[k][me] = sources[k][...] if mode == "gather" else sources[k][me]
        for copy in copies:
            copy.wait()

    shapes = []
    for array, axis, mode in arrays:
        shape = (sizes[axis],) + array.shape if mode == "gather" else array.shape
        shapes.append(jax.ShapeDtypeStruct(shape, array.dtype))
    return pl.pallas_call(
        kernel,
        out_shape=shapes,
        in_specs=[pl.BlockSpec(memory_space=pltpu.VMEM)] * count,
        out_specs=[pl.BlockSpec(memory_space=pltpu.VMEM)] * count,
        scratch_shapes=[
            pltpu.SemaphoreType.DMA((count, widest)),
            pltpu.SemaphoreType.DMA((count, widest)),
        ],
        compiler_params=pltpu.CompilerParams(collective_id=collective_id, has_side_effects=True),
    )(*[array for array, _, _ in arrays])


def split_three(values):
    high = values.astype(jnp.bfloat16).astype(jnp.float32)
    rest = values - high
    middle = rest.astype(jnp.bfloat16).astype(jnp.float32)
    return high, middle, rest - middle


def feature_rows(points, left):
    high, middle, low = split_three(points)
    norms = split_three(jnp.sum(points * points, axis=0, keepdims=True))
    row = lax.broadcasted_iota(jnp.int32, points.shape, 0)
    first = 0 if left else 3
    tail = jnp.where(row < 6, 1.0, 0.0)
    for k in range(3):
        tail = jnp.where(row == first + k, norms[k], tail)
    if left:
        parts = [-2.0 * part for part in (high, high, middle, middle, high, low)]
    else:
        parts = [high, middle, high, middle, low, high]
    parts += [tail, jnp.zeros_like(tail)]
    return jnp.concatenate(parts, axis=0)


def tile_kernel(tile, left_points, right_points, vectors, out_ref, left, right):
    rows, _, own_count = right_points.shape
    per_block = own_count // tile

    @pl.when(pl.program_id(0) == 0)
    def _():
        def build(index, carry):
            features = feature_rows(right_points[index], False)
            start = pl.multiple_of(index * own_count, own_count)
            right[pl.ds(start, own_count), :] = jnp.transpose(features).astype(jnp.bfloat16)
            return carry

        lax.fori_loop(0, rows, build, 0)

    left[...] = feature_rows(left_points[0], True).astype(jnp.bfloat16)
    out_ref[...] = jnp.zeros_like(out_ref)

    def step(index, carry):
        start = pl.multiple_of(index * tile, tile)
        squared = jnp.dot(
            right[pl.ds(start, tile), :], left[...], preferred_element_type=jnp.float32
        )
        squared = jnp.maximum(squared, 1e-30)
        radius = squared * lax.rsqrt(squared)
        shifted = radius + SHIFT
        kernel = ((shifted * shifted + LIFT) * jnp.exp2(EXPONENT - radius)).astype(jnp.bfloat16)
        inner = pl.multiple_of(lax.rem(index, per_block) * tile, tile)
        out_ref[0] += jnp.dot(
            vectors[index // per_block, :, pl.ds(inner, tile)],
            kernel,
            preferred_element_type=jnp.float32,
        )
        return carry

    lax.fori_loop(0, rows * per_block, step, 0)


def apply_tile(left_points, right_points, vectors):
    cols, dims, own_count = left_points.shape
    rows, probes, _ = vectors.shape
    tile = math.gcd(512, own_count)

    def kernel(*refs):
        tile_kernel(tile, *refs)

    return pl.pallas_call(
        kernel,
        grid=(cols,),
        out_shape=jax.ShapeDtypeStruct((cols, probes, own_count), jnp.float32),
        in_specs=[
            pl.BlockSpec((1, dims, own_count), lambda i: (i, 0, 0)),
            pl.BlockSpec((rows, dims, own_count), lambda i: (0, 0, 0)),
            pl.BlockSpec((rows, probes, own_count), lambda i: (0, 0, 0)),
        ],
        out_specs=pl.BlockSpec((1, probes, own_count), lambda i: (i, 0, 0)),
        scratch_shapes=[
            pltpu.VMEM((FEATURES, own_count), jnp.bfloat16),
            pltpu.VMEM((rows * own_count, FEATURES), jnp.bfloat16),
        ],
    )(left_points, right_points, vectors)


def greet(sizes):
    barrier = pltpu.get_barrier_semaphore()
    for axis, size in sizes.items():
        me = lax.axis_index(axis)
        for offset in range(1, size):
            pl.semaphore_signal(
                barrier,
                inc=1,
                device_id={axis: lax.rem(me + offset, size)},
                device_id_type=MESH,
            )
    pl.semaphore_wait(barrier, sum(size - 1 for size in sizes.values()))


def push(source, target, send_sem, recv_sem, axis, peer):
    copy = pltpu.make_async_remote_copy(
        src_ref=source,
        dst_ref=target,
        send_sem=send_sem,
        recv_sem=recv_sem,
        device_id={axis: peer},
        device_id_type=MESH,
    )
    copy.start()
    return copy


def spread(source, target, send_sem, recv_sem, axis, size):
    me = lax.axis_index(axis)
    return [
        push(source, target.at[me], send_sem.at[o], recv_sem.at[o], axis, lax.rem(me + o, size))
        for o in range(1, size)
    ]


def total_over(mine, held, send_sem, recv_sem, axis, size):
    copies = spread(mine, held, send_sem, recv_sem, axis, size)
    held[lax.axis_index(axis)] = mine[...]
    for copy in copies:
        copy.wait()
    total = held[0]
    for k in range(1, size):
        total = total + held[k]
    return total


def step_kernel(
    rows,
    cols,
    terms,
    direction,
    residual,
    iterate,
    previous,
    noise,
    new_iterate,
    new_residual,
    everyone,
    parts,
    curve,
    curve_cols,
    curve_rows,
    sems,
    row_sems,
    chip_sems,
    core_sems,
):
    row, col = lax.axis_index("row"), lax.axis_index("col")
    greet({"row": rows, "col": cols})
    copies = [
        push(
            terms.at[lax.rem(col + o, cols)],
            parts.at[col],
            sems.at[0, 0, o],
            sems.at[1, 0, o],
            "col",
            lax.rem(col + o, cols),
        )
        for o in range(1, cols)
    ]
    total = terms[col] + noise[0] * direction[...]
    for o, copy in enumerate(copies, 1):
        copy.wait()
        total = total + parts[lax.rem(col + cols - o, cols)]
    curvature = jnp.sum(direction[...] * total, axis=1, keepdims=True)
    curve[0] = jnp.broadcast_to(curvature, curve.shape[1:])
    curve[1] = total_over(curve.at[0], curve_cols, sems.at[0, 1], sems.at[1, 1], "col", cols)
    curvature = total_over(curve.at[1], curve_rows, sems.at[0, 2], sems.at[1, 2], "row", rows)
    step_size = (previous[...] / curvature)[:, :1]
    new_iterate[...] = iterate[...] + step_size * direction[...]
    updated = residual[...] - step_size * total
    new_residual[...] = updated
    everyone[col, row] = updated.astype(jnp.bfloat16)

    partner = col + 1 - 2 * lax.rem(col, 2)
    waits, row_copies, chip_copies = [], [], []
    for o in range(1, rows):
        slot = everyone.at[col, row]
        row_copies.append(
            push(slot, slot, row_sems.at[0, o], row_sems.at[1, o], "row", lax.rem(row + o, rows))
        )
    chips = cols // 2
    for o in range(rows):
        if o:
            row_copies[o - 1].wait_recv()
        slot = everyone.at[col, lax.rem(row + rows - o, rows)]
        for e in range(1, chips):
            chip_copies.append(
                (
                    o,
                    e,
                    push(
                        slot,
                        slot,
                        chip_sems.at[0, e, o],
                        chip_sems.at[1, e, o],
                        "col",
                        lax.rem(col + 2 * e, cols),
                    ),
                )
            )
        waits.append(
            push(slot, slot, core_sems.at[0, 0, o], core_sems.at[1, 0, o], "col", partner)
        )
    for o, e, copy in chip_copies:
        copy.wait_recv()
        slot = everyone.at[lax.rem(col + cols - 2 * e, cols), lax.rem(row + rows - o, rows)]
        waits.append(
            push(slot, slot, core_sems.at[0, e, o], core_sems.at[1, e, o], "col", partner)
        )
    for copy in row_copies:
        copy.wait_send()
    for _, _, copy in chip_copies:
        copy.wait_send()
    for copy in waits:
        copy.wait()


def take_step(terms, direction, residual, iterate, previous, noise, rows, cols):
    probes, own_count = direction.shape
    widest = max(rows, cols)
    vmem = pl.BlockSpec(memory_space=pltpu.VMEM)

    def kernel(*refs):
        step_kernel(rows, cols, *refs)

    return pl.pallas_call(
        kernel,
        out_shape=[
            jax.ShapeDtypeStruct((probes, own_count), jnp.float32),
            jax.ShapeDtypeStruct((probes, own_count), jnp.float32),
            jax.ShapeDtypeStruct((cols, rows, probes, own_count), jnp.bfloat16),
        ],
        in_specs=[vmem] * 5 + [pl.BlockSpec(memory_space=pltpu.SMEM)],
        out_specs=[vmem] * 3,
        scratch_shapes=[
            pltpu.VMEM((cols, probes, own_count), jnp.float32),
            pltpu.VMEM((2, probes, 128), jnp.float32),
            pltpu.VMEM((cols, probes, 128), jnp.float32),
            pltpu.VMEM((rows, probes, 128), jnp.float32),
            pltpu.SemaphoreType.DMA((2, 3, widest)),
            pltpu.SemaphoreType.DMA((2, rows)),
            pltpu.SemaphoreType.DMA((2, cols // 2, rows)),
            pltpu.SemaphoreType.DMA((2, cols // 2, rows)),
        ],
        compiler_params=pltpu.CompilerParams(collective_id=2, has_side_effects=True),
    )(terms, direction, residual, iterate, previous, noise)


def cluster_kernel(
    rows,
    cols,
    everyone,
    local,
    present,
    origin,
    wanted,
    direction,
    previous,
    factors,
    new_direction,
    rz_out,
    held,
    inner_parts,
    inner_got,
    inner_all,
    outer_cols,
    outgoing,
    incoming,
    rz,
    rz_cols,
    rz_rows,
    load_sems,
    part_sems,
    sems,
):
    row, col = lax.axis_index("row"), lax.axis_index("col")
    slots, length, width = held.shape
    probes, own_count = direction.shape
    parts = CORE // own_count
    pieces = own_count // width
    loads = [
        pltpu.make_async_copy(factors.at[s], held.at[s], load_sems.at[s]) for s in range(slots)
    ]
    for load in loads:
        load.start()
    greet({"row": rows, "col": cols})

    chosen, copies = [], []
    position = lax.broadcasted_iota(jnp.int32, (CORE, width), 0)
    for s in range(slots):
        block = [everyone[origin[0, s] + p, origin[1, s]] for p in range(parts)]
        block = jnp.concatenate(block, axis=1) if parts > 1 else block[0]
        pick = jnp.where(position == local[s : s + 1, :], 1.0, 0.0).astype(jnp.bfloat16)
        values = jnp.dot(block, pick, preferred_element_type=jnp.float32).astype(jnp.bfloat16)
        chosen.append(values)
        loads[s].wait()
        inner = lax.dot_general(
            values, held[s], (((1,), (1,)), ((), ())), preferred_element_type=jnp.float32
        )
        for k in range(cols):
            inner_parts[k, s] = inner[:, k * width : (k + 1) * width]
        for o in range(1, cols):
            peer = lax.rem(col + o, cols)
            copies.append(
                push(
                    inner_parts.at[peer, s],
                    inner_got.at[col, s],
                    part_sems.at[0, s, o],
                    part_sems.at[1, s, o],
                    "col",
                    peer,
                )
            )
    for copy in copies:
        copy.wait()
    for s in range(slots):
        inner = inner_parts[col, s]
        for o in range(1, cols):
            inner = inner + inner_got[lax.rem(col + o, cols), s]
        inner_all[col, s] = (inner * present[s : s + 1, :]).astype(jnp.bfloat16)
    mine = inner_all.at[col]
    for copy in spread(mine, inner_all, sems.at[0, 0], sems.at[1, 0], "col", cols):
        copy.wait()
    rz_part = jnp.zeros((probes, 1), jnp.float32)
    for s in range(slots):
        inner = jnp.concatenate([inner_all[k, s] for k in range(cols)], axis=1)
        outer = jnp.dot(inner, held[s], preferred_element_type=jnp.float32)
        outer_cols[col, s] = outer.astype(jnp.bfloat16)
        rz_part += jnp.sum(chosen[s].astype(jnp.float32) * outer, axis=1, keepdims=True)
    is_core = jnp.where(col * width < CORE, 1.0, 0.0)
    rz[0] = jnp.broadcast_to(rz_part * is_core, rz.shape[1:])
    mine = outer_cols.at[col]
    copies = spread(mine, outer_cols, sems.at[0, 1], sems.at[1, 1], "col", cols)
    rz[1] = total_over(rz.at[0], rz_cols, sems.at[0, 2], sems.at[1, 2], "col", cols)
    for copy in copies:
        copy.wait()
    first = lax.rem(col, parts) * pieces
    for n in range(pieces):
        values = [outer_cols[first + n, s].astype(jnp.float32) for s in range(slots)]
        for r in range(rows):
            total = jnp.zeros((probes, width), jnp.float32)
            for s in range(slots):
                total = total + wanted[r, s] * values[s]
            outgoing[r, n] = total.astype(jnp.bfloat16)
    copies = [
        push(
            outgoing.at[lax.rem(row + o, rows)],
            incoming.at[row],
            sems.at[0, 3, o],
            sems.at[1, 3, o],
            "row",
            lax.rem(row + o, rows),
        )
        for o in range(1, rows)
    ]
    incoming[row] = outgoing[row]
    total = total_over(rz.at[1], rz_rows, sems.at[0, 4], sems.at[1, 4], "row", rows)
    rz_out[...] = total
    ratio = (total / previous[...])[:, :1]
    for copy in copies:
        copy.wait()
    for n in range(pieces):
        precond = incoming[0, n].astype(jnp.float32)
        for r in range(1, rows):
            precond = precond + incoming[r, n].astype(jnp.float32)
        span = slice(n * width, (n + 1) * width)
        new_direction[:, span] = precond + ratio * direction[:, span]


def apply_clusters(everyone, local, present, origin, wanted, direction, previous, factors):
    cols, rows, probes, own_count = everyone.shape
    slots, length, width = factors.shape
    pieces = own_count // width
    widest = max(rows, cols)
    vmem = pl.BlockSpec(memory_space=pltpu.VMEM)
    smem = pl.BlockSpec(memory_space=pltpu.SMEM)

    def kernel(*refs):
        cluster_kernel(rows, cols, *refs)

    return pl.pallas_call(
        kernel,
        out_shape=[
            jax.ShapeDtypeStruct((probes, own_count), jnp.float32),
            jax.ShapeDtypeStruct((probes, 128), jnp.float32),
        ],
        in_specs=[vmem, vmem, vmem, smem, smem, vmem, vmem, pl.BlockSpec(memory_space=pl.ANY)],
        out_specs=[vmem] * 2,
        scratch_shapes=[
            pltpu.VMEM((slots, length, width), jnp.bfloat16),
            pltpu.VMEM((cols, slots, probes, width), jnp.float32),
            pltpu.VMEM((cols, slots, probes, width), jnp.float32),
            pltpu.VMEM((cols, slots, probes, width), jnp.bfloat16),
            pltpu.VMEM((cols, slots, probes, width), jnp.bfloat16),
            pltpu.VMEM((rows, pieces, probes, width), jnp.bfloat16),
            pltpu.VMEM((rows, pieces, probes, width), jnp.bfloat16),
            pltpu.VMEM((2, probes, 128), jnp.float32),
            pltpu.VMEM((cols, probes, 128), jnp.float32),
            pltpu.VMEM((rows, probes, 128), jnp.float32),
            pltpu.SemaphoreType.DMA((slots,)),
            pltpu.SemaphoreType.DMA((2, slots, cols)),
            pltpu.SemaphoreType.DMA((2, 5, widest)),
        ],
        compiler_params=pltpu.CompilerParams(collective_id=3, has_side_effects=True),
    )(everyone, local, present, origin, wanted, direction, previous, factors)


def lanes(values):
    return jnp.broadcast_to(values[:, None], (values.shape[0], 128))


def on_device(
    points,
    lengthscale,
    noise,
    iterate,
    residual,
    direction,
    previous_rz,
    members,
    slot_cluster,
    factors,
):
    own_count = direction.shape[1]
    rows, cols = lax.axis_size("row"), lax.axis_size("col")
    point_count = rows * cols * own_count
    col = lax.axis_index("col")
    own_width = factors.shape[2]
    parts = CORE // own_count

    scaled = points / lengthscale[:, None] * SPREAD
    direction_low = direction.astype(jnp.bfloat16)
    column_points, column_vectors, row_points = exchange(
        [(scaled, "row", "gather"), (direction_low, "row", "gather"), (scaled, "col", "gather")], 1
    )
    terms = apply_tile(row_points, column_points, column_vectors)
    previous = lanes(previous_rz)
    new_iterate, new_residual, everyone = take_step(
        terms, direction, residual, iterate, previous, noise, rows, cols
    )

    slot_cluster, members, _ = lax.optimization_barrier((slot_cluster, members, column_points))
    own_members = lax.dynamic_slice_in_dim(members, col * own_width, own_width, 1)
    own_ids = jnp.take(own_members, slot_cluster, axis=0)
    source = jnp.minimum(jnp.min(own_ids, axis=1), point_count - 1) // CORE
    local = own_ids - source[:, None] * CORE
    present = (own_ids < point_count).astype(jnp.float32)
    first = source * parts
    origin = jnp.stack([first % cols, first // cols])
    devices = jnp.arange(rows, dtype=jnp.int32) * cols + col
    wanted = ((devices // parts)[:, None] == slot_cluster[None, :]).astype(jnp.float32)
    new_direction, rz_lanes = apply_clusters(
        everyone, local, present, origin, wanted, direction, previous, factors
    )
    return (new_iterate, new_residual, new_direction, rz_lanes[:, 0])


def solution(mesh):
    placed = (
        P(None, ("row", "col")),
        P(),
        P(),
        P(None, ("row", "col")),
        P(None, ("row", "col")),
        P(None, ("row", "col")),
        P(),
        P(),
        P("row"),
        P("row", None, "col"),
    )
    return jax.shard_map(
        on_device,
        mesh=mesh,
        in_specs=placed,
        out_specs=(P(None, ("row", "col")), P(None, ("row", "col")), P(None, ("row", "col")), P()),
        check_vma=False,
    )
```

time: 686 us -> 166 us (0.24)
  matrix products: 228 us -> 0 us
  blocking collectives: 164 us -> 0 us
  Pallas kernels: 0 us -> 151 us
  other arithmetic: 130 us -> 7.79 us
  waiting for transfers between devices: 76 us -> 0 us
  local copies, waits for them, and re-layouts: 63.6 us -> 5.97 us
  between operations: 15 us -> 1.37 us
  starting transfers between devices: 9.04 us -> 0 us
    dot_general x4 -> x0, matrix products: 228 us -> none  [the longest x1 191 us: kernel_block(): lax.dot_general(left_points, right_points, (((0,), (0,)), ((), ())), prec...]
    pallas_call x0 -> x4, Pallas kernels: none -> 151 us  [the longest x1 68.4 us: apply_tile(): pl.pallas_call(kernel, grid=(cols,), out_shape=jax.ShapeDtypeStruct((cols...]
    scatter-add x1 -> x0, other arithmetic: 112 us -> none  [on_device(): jnp.zeros((own_count + 1, probes), jnp.float32).at[local_ids].add(received)]
    psum x3 -> x0, blocking collectives: 94.9 us -> none  [the longest x1 39.3 us: on_device(): lax.psum(jnp.sum(direction * kernel_image, axis=1), ('row', 'col'))]
    all_gather x3 -> x0, blocking collectives: 68.8 us -> none  [the longest x1 31.6 us: on_device(): lax.all_gather(scaled, 'row', axis=1, tiled=True)]
    all_to_all x2 -> x0, waiting for transfers between devices: 33.6 us -> none  [the longest x1 26.1 us: on_device(): lax.all_to_all(send_values, ('row', 'col'), split_axis=0, concat_axis=0,...]
    all_gather x1 -> x0, waiting for transfers between devices: 22.9 us -> none  [on_device(): gathered = lax.all_gather(residual_low, ('row', 'col'), axis=1, tiled=True)]
    reduce_scatter x1 -> x0, waiting for transfers between devices: 19.5 us -> none  [on_device(): lax.psum_scatter(column_terms, 'col', scatter_dimension=1, tiled=True)]
  transfers between devices with their start and end apart: 4 -> 0, of which waited for: 4 -> 0; matrix products, arithmetic and copies ran while one was open for 3% -> 0% of each run, Pallas kernels for 0% -> 0%
where the time goes in v1:
time: 166 us
  Pallas kernels  151 us (91%)
  other arithmetic  7.79 us (5%)
  local copies, waits for them, and re-layouts  5.97 us (4%)
    pallas_call x1, Pallas kernels, apply_tile(): pl.pallas_call(kernel, grid=(cols,), out_shape=jax.ShapeDtypeStruct((cols...  68.4 us
    pallas_call x1, Pallas kernels, apply_clusters(): pl.pallas_call(kernel, out_shape=[jax.ShapeDtypeStruct((probes, own_count...  34 us
    pallas_call x1, Pallas kernels, take_step(): pl.pallas_call(kernel, out_shape=[jax.ShapeDtypeStruct((probes, own_count...  31 us
    pallas_call x1, Pallas kernels, exchange(): pl.pallas_call(kernel, out_shape=shapes, in_specs=[pl.BlockSpec(memory_sp...  17.3 us

profile of v1, /device:TPU:0, one launch (start us, length us, event | category | flops | bytes accessed | tf_op | source)
XLA Modules:
  0.0 165.8 jit_solution(18219002440934537082)
XLA Ops:
  0.6 0.0 copy-start
  0.6 1.5 convert_element_type.9.refs_1_
  2.2 1.5 divide_multiply_fusion.refs_0_.refs_2_
  3.6 17.3 %shard_map.129 = (f32[8,8,1024]{2,1,0:T(8,128)}, bf16[8,16,1024]{2,1,0:T(8,128)(2,1)}, f32[4,8,1024]{2,1,0:T(8,128)}) custom-call(f32[8,1024]{1,0:T(8,128)} %divide_multiply_fusion.refs_0_.refs_2_, bf16[16,1024]{1,0:T(8,128)(2,1)} %convert_element_type.9.refs_1_, f32[8,1024]{1,0:T(8,128)} %divide_multiply_fusion.refs_0_.refs_2_), custom_call_target="tpu_custom_call" | custom-call | tf_op jit(solution)/shard_map/pallas_call | solution.py:67
  20.9 0.0 copy-done
  21.0 0.7 compare_select_fusion
  21.6 0.6 gather_fusion
  22.2 0.7 compare_and_fusion
  22.9 0.2 select_reduce_fusion
  23.1 0.6 pad_add_fusion.refs_3_
  23.7 0.7 select_subtract_fusion.refs_1_
  24.4 0.7 compare_convert_fusion.refs_2_
  25.0 68.4 %shard_map.130.refs_0_ = f32[4,16,1024]{2,1,0:T(8,128)} custom-call(f32[4,8,1024]{2,1,0:T(8,128)} %get-tuple-element.14.refs_0_, f32[8,8,1024]{2,1,0:T(8,128)} %get-tuple-element.15.refs_1_, bf16[8,16,1024]{2,1,0:T(8,128)(2,1)} %get-tuple-element.16.refs_2_), custom_call_target="tpu_custom_call" | custom-call | tf_op jit(solution)/shard_map/pallas_call | solution.py:148
  93.4 1.3 broadcast_in_dim.22.refs_4_.refs_6_
  95.4 31.0 %shard_map.131 = (f32[16,1024]{1,0:T(8,128)}, f32[16,1024]{1,0:T(8,128)}, bf16[4,8,16,1024]{3,2,1,0:T(8,128)(2,1)}) custom-call(f32[4,16,1024]{2,1,0:T(8,128)} %shard_map.130.refs_0_, f32[16,1024]{1,0:T(8,128)} %refs_5_.2, f32[16,1024]{1,0:T(8,128)} %refs_2_.1, f32[16,1024]{1,0:T(8,128)} %refs_3_.1, f32[16,128]{1,0:T(8,128)} %broadcast_in_dim.22.refs_4_.refs_6_, ...), custom_call_target="tpu_custom_call" | custom-call | tf_op jit(solution)/shard_map/pallas_call | solution.py:311
  126.4 0.0 copy-start.2
  126.4 0.0 copy-start.1
  126.4 1.4 compare_convert_fusion.1.refs_4_
  127.7 34.0 %shard_map.132 = (f32[16,1024]{1,0:T(8,128)}, f32[16,128]{1,0:T(8,128)}) custom-call(bf16[4,8,16,1024]{3,2,1,0:T(8,128)(2,1)} %get-tuple-element.19.refs_0_, s32[4,512]{1,0:T(4,128)} %select_subtract_fusion.refs_1_, f32[4,512]{1,0:T(4,128)} %compare_convert_fusion.refs_2_, s32[2,4]{1,0:T(2,128)} %pad_add_fusion.refs_3_, ...), custom_call_target="tpu_custom_call" | custom-call | tf_op jit(solution)/shard_map/pallas_call | solution.py:466
  161.7 1.3 slice_reduce_fusion
  163.0 0.0 copy-done.2
  163.0 0.6 copy.18
  163.7 0.0 copy-done.1
  163.7 0.6 copy.19
  164.3 1.5 copy.20
  (5 shorter events, 0.1 us)
Async XLA Ops:
  0.6 20.3 %copy-start = (s32[32,2048]{1,0:T(8,128)S(1)}, s32[32,2048]{1,0:T(8,128)}, u32[]{:S(2)}) copy-start(s32[32,2048]{1,0:T(8,128)} %param.17) | copy-start | bytes 786436
  126.4 36.7 %copy-start.2 = (f32[16,1024]{1,0:T(8,128)S(1)}, f32[16,1024]{1,0:T(8,128)}, u32[]{:S(2)}) copy-start(f32[16,1024]{1,0:T(8,128)} %get-tuple-element.30) | copy-start | bytes 196612
  126.4 37.3 %copy-start.1 = (f32[16,1024]{1,0:T(8,128)S(1)}, f32[16,1024]{1,0:T(8,128)}, u32[]{:S(2)}) copy-start(f32[16,1024]{1,0:T(8,128)} %get-tuple-element.31) | copy-start | bytes 196612

commit v2 on v1

--- a/solution.py
+++ b/solution.py
@@ -100,66 +100,95 @@
     return jnp.concatenate(parts, axis=0)
 
 
-def tile_kernel(tile, left_points, right_points, vectors, out_ref, left, right):
-    rows, _, own_count = right_points.shape
+def tile_kernel(
+    tile, left_points, right_points, left_vectors, right_vectors, out_left, out_right, *scratch
+):
+    left, right, flipped, sums = scratch
+    row, col = lax.axis_index("row"), lax.axis_index("col")
+    cols, _, own_count = left_points.shape
+    rows = right_points.shape[0]
+    half = rows // 2
     per_block = own_count // tile
 
-    @pl.when(pl.program_id(0) == 0)
-    def _():
-        def build(index, carry):
-            features = feature_rows(right_points[index], False)
-            start = pl.multiple_of(index * own_count, own_count)
-            right[pl.ds(start, own_count), :] = jnp.transpose(features).astype(jnp.bfloat16)
-            return carry
-
-        lax.fori_loop(0, rows, build, 0)
-
-    left[...] = feature_rows(left_points[0], True).astype(jnp.bfloat16)
-    out_ref[...] = jnp.zeros_like(out_ref)
-
-    def step(index, carry):
-        start = pl.multiple_of(index * tile, tile)
+    def build_left(c, carry):
+        left[c] = feature_rows(left_points[c], True).astype(jnp.bfloat16)
+        flipped[c] = jnp.transpose(left_vectors[c].astype(jnp.float32)).astype(jnp.bfloat16)
+        return carry
+
+    def build_right(ahead, carry):
+        features = feature_rows(right_points[lax.rem(row + ahead, rows)], False)
+        right[ahead] = jnp.transpose(features).astype(jnp.bfloat16)
+        return carry
+
+    lax.fori_loop(0, cols, build_left, 0)
+    lax.fori_loop(0, half + 1, build_right, 0)
+    out_left[...] = jnp.zeros_like(out_left)
+    sums[...] = jnp.zeros_like(sums)
+
+    def apply(c, ahead, part, both):
+        start = pl.multiple_of(part * tile, tile)
         squared = jnp.dot(
-            right[pl.ds(start, tile), :], left[...], preferred_element_type=jnp.float32
+            right[ahead, pl.ds(start, tile), :], left[c], preferred_element_type=jnp.float32
         )
         squared = jnp.maximum(squared, 1e-30)
         radius = squared * lax.rsqrt(squared)
         shifted = radius + SHIFT
         kernel = ((shifted * shifted + LIFT) * jnp.exp2(EXPONENT - radius)).astype(jnp.bfloat16)
-        inner = pl.multiple_of(lax.rem(index, per_block) * tile, tile)
-        out_ref[0] += jnp.dot(
-            vectors[index // per_block, :, pl.ds(inner, tile)],
+        out_left[c] += jnp.dot(
+            right_vectors[lax.rem(row + ahead, rows), :, pl.ds(start, tile)],
             kernel,
             preferred_element_type=jnp.float32,
         )
+        other = jnp.dot(kernel, flipped[c], preferred_element_type=jnp.float32)
+        sums[ahead, pl.ds(start, tile), :] += both * other
+
+    def step(index, carry):
+        pair, part = index // per_block, lax.rem(index, per_block)
+        c, ahead = lax.rem(pair, cols), pair // cols
+        ahead = jnp.where(ahead > 0, ahead, jnp.where(c <= col, 0, half))
+        same = jnp.logical_and(ahead == 0, c == col)
+        apply(c, ahead, part, jnp.where(same, 0.0, 1.0))
         return carry
 
-    lax.fori_loop(0, rows * per_block, step, 0)
-
-
-def apply_tile(left_points, right_points, vectors):
-    cols, dims, own_count = left_points.shape
-    rows, probes, _ = vectors.shape
-    tile = math.gcd(512, own_count)
+    lax.fori_loop(0, half * cols * per_block, step, 0)
+
+    @pl.when(row < half)
+    def _():
+        def last(part, carry):
+            apply(col, half, part, 1.0)
+            return carry
+
+        lax.fori_loop(0, per_block, last, 0)
+
+    for ahead in range(half + 1):
+        out_right[ahead] = jnp.transpose(sums[ahead])
+
+
+def apply_tile(left_points, right_points, left_vectors, right_vectors):
+    cols, probes, own_count = left_vectors.shape
+    rows = right_vectors.shape[0]
+    half = rows // 2
+    tile = math.gcd(1024, own_count)
+    vmem = pl.BlockSpec(memory_space=pltpu.VMEM)
 
     def kernel(*refs):
         tile_kernel(tile, *refs)
 
     return pl.pallas_call(
         kernel,
-        grid=(cols,),
-        out_shape=jax.ShapeDtypeStruct((cols, probes, own_count), jnp.float32),
-        in_specs=[
-            pl.BlockSpec((1, dims, own_count), lambda i: (i, 0, 0)),
-            pl.BlockSpec((rows, dims, own_count), lambda i: (0, 0, 0)),
-            pl.BlockSpec((rows, probes, own_count), lambda i: (0, 0, 0)),
-        ],
-        out_specs=pl.BlockSpec((1, probes, own_count), lambda i: (i, 0, 0)),
+        out_shape=[
+            jax.ShapeDtypeStruct((cols, probes, own_count), jnp.float32),
+            jax.ShapeDtypeStruct((half + 1, probes, own_count), jnp.float32),
+        ],
+        in_specs=[vmem] * 4,
+        out_specs=[vmem] * 2,
         scratch_shapes=[
-            pltpu.VMEM((FEATURES, own_count), jnp.bfloat16),
-            pltpu.VMEM((rows * own_count, FEATURES), jnp.bfloat16),
-        ],
-    )(left_points, right_points, vectors)
+            pltpu.VMEM((cols, FEATURES, own_count), jnp.bfloat16),
+            pltpu.VMEM((half + 1, own_count, FEATURES), jnp.bfloat16),
+            pltpu.VMEM((cols, own_count, probes), jnp.bfloat16),
+            pltpu.VMEM((half + 1, own_count, probes), jnp.float32),
+        ],
+    )(left_points, right_points, left_vectors, right_vectors)
 
 
 def greet(sizes):
@@ -212,6 +241,7 @@
     rows,
     cols,
     terms,
+    others,
     direction,
     residual,
     iterate,
@@ -221,6 +251,7 @@
     new_residual,
     everyone,
     parts,
+    other_parts,
     curve,
     curve_cols,
     curve_rows,
@@ -242,10 +273,24 @@
         )
         for o in range(1, cols)
     ]
-    total = terms[col] + noise[0] * direction[...]
+    other_copies = [
+        push(
+            others.at[ahead],
+            other_parts.at[ahead],
+            sems.at[0, 3, ahead],
+            sems.at[1, 3, ahead],
+            "row",
+            lax.rem(row + ahead, rows),
+        )
+        for ahead in range(1, rows // 2 + 1)
+    ]
+    total = terms[col] + others[0] + noise[0] * direction[...]
     for o, copy in enumerate(copies, 1):
         copy.wait()
         total = total + parts[lax.rem(col + cols - o, cols)]
+    for ahead, copy in enumerate(other_copies, 1):
+        copy.wait()
+        total = total + other_parts[ahead]
     curvature = jnp.sum(direction[...] * total, axis=1, keepdims=True)
     curve[0] = jnp.broadcast_to(curvature, curve.shape[1:])
     curve[1] = total_over(curve.at[0], curve_cols, sems.at[0, 1], sems.at[1, 1], "col", cols)
@@ -300,7 +345,7 @@
         copy.wait()
 
 
-def take_step(terms, direction, residual, iterate, previous, noise, rows, cols):
+def take_step(terms, others, direction, residual, iterate, previous, noise, rows, cols):
     probes, own_count = direction.shape
     widest = max(rows, cols)
     vmem = pl.BlockSpec(memory_space=pltpu.VMEM)
@@ -315,20 +360,21 @@
             jax.ShapeDtypeStruct((probes, own_count), jnp.float32),
             jax.ShapeDtypeStruct((cols, rows, probes, own_count), jnp.bfloat16),
         ],
-        in_specs=[vmem] * 5 + [pl.BlockSpec(memory_space=pltpu.SMEM)],
+        in_specs=[vmem] * 6 + [pl.BlockSpec(memory_space=pltpu.SMEM)],
         out_specs=[vmem] * 3,
         scratch_shapes=[
             pltpu.VMEM((cols, probes, own_count), jnp.float32),
+            pltpu.VMEM(others.shape, jnp.float32),
             pltpu.VMEM((2, probes, 128), jnp.float32),
             pltpu.VMEM((cols, probes, 128), jnp.float32),
             pltpu.VMEM((rows, probes, 128), jnp.float32),
-            pltpu.SemaphoreType.DMA((2, 3, widest)),
+            pltpu.SemaphoreType.DMA((2, 4, widest)),
             pltpu.SemaphoreType.DMA((2, rows)),
             pltpu.SemaphoreType.DMA((2, cols // 2, rows)),
             pltpu.SemaphoreType.DMA((2, cols // 2, rows)),
         ],
         compiler_params=pltpu.CompilerParams(collective_id=2, has_side_effects=True),
-    )(terms, direction, residual, iterate, previous, noise)
+    )(terms, others, direction, residual, iterate, previous, noise)
 
 
 def cluster_kernel(
@@ -515,13 +561,19 @@
 
     scaled = points / lengthscale[:, None] * SPREAD
     direction_low = direction.astype(jnp.bfloat16)
-    column_points, column_vectors, row_points = exchange(
-        [(scaled, "row", "gather"), (direction_low, "row", "gather"), (scaled, "col", "gather")], 1
+    column_points, column_vectors, row_points, row_vectors = exchange(
+        [
+            (scaled, "row", "gather"),
+            (direction_low, "row", "gather"),
+            (scaled, "col", "gather"),
+            (direction_low, "col", "gather"),
+        ],
+        1,
     )
-    terms = apply_tile(row_points, column_points, column_vectors)
+    terms, others = apply_tile(row_points, column_points, row_vectors, column_vectors)
     previous = lanes(previous_rz)
     new_iterate, new_residual, everyone = take_step(
-        terms, direction, residual, iterate, previous, noise, rows, cols
+        terms, others, direction, residual, iterate, previous, noise, rows, cols
     )
 
     slot_cluster, members, _ = lax.optimization_barrier((slot_cluster, members, column_points))

time: 166 us -> 145 us (0.87)
  Pallas kernels: 151 us -> 129 us
    pallas_call x1, Pallas kernels: 68.4 us -> 41 us  [apply_tile(): pl.pallas_call(kernel, out_shape=[jax.ShapeDtypeStruct((cols, probes, own...]
    pallas_call x1, Pallas kernels: 31 us -> 36.1 us  [take_step(): pl.pallas_call(kernel, out_shape=[jax.ShapeDtypeStruct((probes, own_count...]
where the time goes in v2:
time: 145 us; the launch traced here: 144 us
  Pallas kernels  129 us (89%)
  other arithmetic  7.81 us (5%)
  local copies, waits for them, and re-layouts  5.97 us (4%)
    pallas_call x1, Pallas kernels, apply_tile(): pl.pallas_call(kernel, out_shape=[jax.ShapeDtypeStruct((cols, probes, own...  41 us
    pallas_call x1, Pallas kernels, take_step(): pl.pallas_call(kernel, out_shape=[jax.ShapeDtypeStruct((probes, own_count...  36.1 us
    pallas_call x1, Pallas kernels, apply_clusters(): pl.pallas_call(kernel, out_shape=[jax.ShapeDtypeStruct((probes, own_count...  34.4 us
    pallas_call x1, Pallas kernels, exchange(): pl.pallas_call(kernel, out_shape=shapes, in_specs=[pl.BlockSpec(memory_sp...  17.5 us

profile of v2, /device:TPU:0, one launch (start us, length us, event | category | flops | bytes accessed | tf_op | source)
XLA Modules:
  0.0 144.2 jit_solution(306188192370592587)
XLA Ops:
  0.6 0.0 copy-start
  0.6 1.5 %convert_element_type.9.refs_1_.refs_3_ = bf16[16,1024]{1,0:T(8,128)(2,1)} convert(f32[16,1024]{1,0:T(8,128)} %refs_5_.1) | non-fusion elementwise | flops 16384 | bytes 98304 | tf_op jit(solution)/shard_map/convert_element_type | solution.py:563
  2.2 1.5 %divide_multiply_fusion.refs_0_.refs_2_ = f32[8,1024]{1,0:T(8,128)} fusion(f32[8,1024]{1,0:T(8,128)} %param.10, f32[8]{0:T(128)} %param.11), kind=kLoop, calls=%fused_computation.1 | loop fusion | flops 16384 | bytes 65568 | tf_op jit(solution)/shard_map/mul | solution.py:562
  3.6 17.5 %shard_map.129 = (f32[8,8,1024]{2,1,0:T(8,128)}, bf16[8,16,1024]{2,1,0:T(8,128)(2,1)}, f32[4,8,1024]{2,1,0:T(8,128)}, bf16[4,16,1024]{2,1,0:T(8,128)(2,1)}) custom-call(f32[8,1024]{1,0:T(8,128)} %divide_multiply_fusion.refs_0_.refs_2_, bf16[16,1024]{1,0:T(8,128)(2,1)} %convert_element_type.9.refs_1_.refs_3_, f32[8,1024]{1,0:T(8,128)} %divide_multiply_fusion.refs_0_.refs_2_, ...), custom_call_target="tpu_custom_call" | custom-call | tf_op jit(solution)/shard_map/pallas_call | solution.py:67
  21.2 0.0 copy-done
  21.2 0.7 compare_select_fusion
  21.9 0.6 gather_fusion
  22.4 0.7 compare_and_fusion
  23.1 0.2 select_reduce_fusion
  23.3 0.6 pad_add_fusion.refs_3_
  23.9 0.7 select_subtract_fusion.refs_1_
  24.6 0.7 compare_convert_fusion.refs_2_
  25.3 41.0 %shard_map.130 = (f32[4,16,1024]{2,1,0:T(8,128)}, f32[5,16,1024]{2,1,0:T(8,128)}) custom-call(f32[4,8,1024]{2,1,0:T(8,128)} %get-tuple-element.17.refs_0_, f32[8,8,1024]{2,1,0:T(8,128)} %get-tuple-element.18.refs_1_, bf16[4,16,1024]{2,1,0:T(8,128)(2,1)} %get-tuple-element.19.refs_2_, bf16[8,16,1024]{2,1,0:T(8,128)(2,1)} %get-tuple-element.20.refs_3_), custom_call_target="tpu_custom_call" | custom-call | tf_op jit(solution)/shard_map/pallas_call | solution.py:177
  66.3 1.3 broadcast_in_dim.22.refs_5_.refs_6_
  68.3 36.1 %shard_map.131 = (f32[16,1024]{1,0:T(8,128)}, f32[16,1024]{1,0:T(8,128)}, bf16[4,8,16,1024]{3,2,1,0:T(8,128)(2,1)}) custom-call(f32[4,16,1024]{2,1,0:T(8,128)} %get-tuple-element.21.refs_0_, f32[5,16,1024]{2,1,0:T(8,128)} %get-tuple-element.22.refs_1_, f32[16,1024]{1,0:T(8,128)} %refs_5_.1, f32[16,1024]{1,0:T(8,128)} %refs_3_.1, f32[16,1024]{1,0:T(8,128)} %refs_4_.1, ...), custom_call_target="tpu_custom_call" | custom-call | tf_op jit(solution)/shard_map/pallas_call | solution.py:356
  104.3 0.0 copy-start.2
  104.3 0.0 copy-start.1
  104.4 1.3 compare_convert_fusion.1.refs_4_
  105.7 34.4 %shard_map.132 = (f32[16,1024]{1,0:T(8,128)}, f32[16,128]{1,0:T(8,128)}) custom-call(bf16[4,8,16,1024]{3,2,1,0:T(8,128)(2,1)} %get-tuple-element.25.refs_0_, s32[4,512]{1,0:T(4,128)} %select_subtract_fusion.refs_1_, f32[4,512]{1,0:T(4,128)} %compare_convert_fusion.refs_2_, s32[2,4]{1,0:T(2,128)} %pad_add_fusion.refs_3_, ...), custom_call_target="tpu_custom_call" | custom-call | tf_op jit(solution)/shard_map/pallas_call | solution.py:512
  140.1 1.3 slice_reduce_fusion
  141.5 0.0 copy-done.2
  141.5 0.6 copy.18
  142.1 0.0 copy-done.1
  142.1 0.6 copy.19
  142.7 1.5 %copy.20 = f32[16,1024]{1,0:T(8,128)} copy(f32[16,1024]{1,0:T(8,128)} %get-tuple-element.38) | data formatting | bytes 131072
  (5 shorter events, 0.1 us)
Async XLA Ops:
  0.6 20.5 %copy-start = (s32[32,2048]{1,0:T(8,128)S(1)}, s32[32,2048]{1,0:T(8,128)}, u32[]{:S(2)}) copy-start(s32[32,2048]{1,0:T(8,128)} %param.17) | copy-start | bytes 786436
  104.3 37.1 %copy-start.2 = (f32[16,1024]{1,0:T(8,128)S(1)}, f32[16,1024]{1,0:T(8,128)}, u32[]{:S(2)}) copy-start(f32[16,1024]{1,0:T(8,128)} %get-tuple-element.36) | copy-start | bytes 196612
  104.3 37.8 %copy-start.1 = (f32[16,1024]{1,0:T(8,128)S(1)}, f32[16,1024]{1,0:T(8,128)}, u32[]{:S(2)}) copy-start(f32[16,1024]{1,0:T(8,128)} %get-tuple-element.37) | copy-start | bytes 196612
